TPU v7x, 32 devices: a whole 2x2x4 slice. The times are simulated.
32 devices in a mesh: crops: 2 (over y), rows: 4 (over z), chan: 2 (over x), sub: 2 (over core).
Axes of the slice: x: 2, y: 2, z: 4, core: 2. Of those that a mesh axis runs over, the one named last changes fastest.
Arguments:
- pair: bfloat16 [64, 32, 128], P(('crops', 'rows', 'sub')), parts along dimension 0, may hold values from -6 to 6
- residue_mask: int32 [64], P('crops'), parts along dimension 0, may hold values from 0 to 1, as said below
- in_gain: float32 [2, 128], replicated, may hold values from 0.1 to 1.9
- in_bias: float32 [2, 128], replicated, may hold values from -3 to 3
- projections: bfloat16 [2, 4, 128, 128], P(None, None, None, 'chan'), may hold values from -0.5 to 0.5
- gate_weight: bfloat16 [2, 128, 128], replicated, may hold values from -0.5 to 0.5
- out_gain: float32 [2, 128], replicated, may hold values from 0.1 to 1.9
- out_bias: float32 [2, 128], replicated, may hold values from -3 to 3
- out_weight: bfloat16 [2, 128, 128], replicated, may hold values from -0.5 to 0.5
Outputs:
- pair_out: bfloat16 [64, 32, 128], P(('crops', 'rows', 'sub'), 'chan'), parts along dimension 0
There are 2 independent parts, one for each index of `crops`. A program takes and returns all parts, laid end to end along the dimension named above; an argument that names none is the same for every part. Nothing has to cross between parts.
Inputs may be any that keep to these rules, and one draw needn't show every extreme that they name: `residue_mask`: residue 0 is always present and residue 32 - 1 is always a gap or padding.
All inputs are finite; a program needn't handle non-finite values.
Results may differ from a plain program's by a relative error of at most 0.012.
Values may be sent and summed in bfloat16 or wider, within the bound.
A program may use at most 64 MiB of HBM per device.

v0:
```python
import jax
import jax.numpy as jnp
from jax import lax
from jax.sharding import PartitionSpec as P

epsilon = 1e-05


def normalize(values, reduce_axis):
    centre = jnp.mean(values, axis=reduce_axis, keepdims=True)
    centred = values - centre
    spread = jnp.mean(centred * centred, axis=reduce_axis, keepdims=True)
    return centred * lax.rsqrt(spread + epsilon)


def shards(
    pair, residue_mask, in_gain, in_bias, projections, gate_weight, out_gain, out_bias, out_weight
):
    rows_block = pair.shape[0]
    length = pair.shape[1]
    chan_count = lax.axis_size("chan")
    chan_index = lax.axis_index("chan")
    quarter = length // chan_count
    row_start = lax.axis_index(("rows", "sub")) * rows_block
    mask_float = residue_mask.astype(jnp.float32)
    own_mask = lax.dynamic_slice_in_dim(mask_float, row_start, rows_block)
    pair_mask = own_mask[None, :, None] * mask_float[None, None, :]

    def project(full_rows, layer_index):
        normed = (
            normalize(full_rows.astype(jnp.float32), 2) * in_gain[layer_index]
            + in_bias[layer_index]
        ).astype(jnp.bfloat16)
        projected = jnp.einsum(
            "ikc,qch->qhik", normed, projections[layer_index], preferred_element_type=jnp.float32
        )
        left_edges = (jax.nn.sigmoid(projected[0]) * projected[1] * pair_mask).astype(jnp.bfloat16)
        right_edges = (jax.nn.sigmoid(projected[2]) * projected[3] * pair_mask).astype(jnp.bfloat16)
        return (normed, left_edges, right_edges)

    def finish(triangle, normed, residual, layer_index):
        gathered = lax.all_to_all(triangle, "chan", split_axis=2, concat_axis=0, tiled=True)
        whole_float = gathered.astype(jnp.float32)
        scaled = (
            normalize(whole_float, 0) * out_gain[layer_index][:, None, None]
            + out_bias[layer_index][:, None, None]
        ).astype(jnp.bfloat16)
        update = jnp.einsum(
            "hij,hc->ijc", scaled, out_weight[layer_index], preferred_element_type=jnp.float32
        )
        normed_part = lax.dynamic_slice_in_dim(normed, chan_index * quarter, quarter, 1)
        gating = jax.nn.sigmoid(
            jnp.einsum(
                "ijc,cd->ijd",
                normed_part,
                gate_weight[layer_index],
                preferred_element_type=jnp.float32,
            )
        )
        return (residual.astype(jnp.float32) + gating * update).astype(jnp.bfloat16)

    normed, left_edges, right_edges = project(pair, 0)
    triangle = jnp.einsum(
        "hik,hjk->hij",
        left_edges,
        lax.all_gather(right_edges, ("rows", "sub"), axis=1, tiled=True),
        preferred_element_type=jnp.float32,
    ).astype(jnp.bfloat16)
    own_quarter = lax.dynamic_slice_in_dim(pair, chan_index * quarter, quarter, 1)
    layer_one = finish(triangle, normed, own_quarter, 0)
    full_rows = lax.all_gather(layer_one, "chan", axis=1, tiled=True)
    normed, left_edges, right_edges = project(full_rows, 1)
    left_cols, right_cols = (
        lax.all_to_all(left_edges, ("rows", "sub"), split_axis=2, concat_axis=1, tiled=True),
        lax.all_to_all(right_edges, ("rows", "sub"), split_axis=2, concat_axis=1, tiled=True),
    )
    triangle = jnp.einsum(
        "hki,hkj->hij",
        left_cols,
        lax.all_gather(right_cols, ("rows", "sub"), axis=2, tiled=True),
        preferred_element_type=jnp.float32,
    )
    return finish(triangle.astype(jnp.bfloat16), normed, layer_one, 1)


def solution(mesh):
    placed = (
        P(("crops", "rows", "sub"), None, None),
        P("crops"),
        P(),
        P(),
        P(None, None, None, "chan"),
        P(),
        P(),
        P(),
        P(),
    )
    return jax.shard_map(
        shards,
        mesh=mesh,
        in_specs=placed,
        out_specs=P(("crops", "rows", "sub"), "chan", None),
        check_vma=False,
    )
```

profile of v0, /device:TPU:0, one launch (start us, length us, event | category | flops | bytes accessed | tf_op | source)
XLA Modules:
  0.0 73.9 jit_solution(12154159398881067945)
XLA Ops:
  0.0 0.6 copy-done.8
  0.8 0.8 %convert_reduce_fusion.1 = f32[4,32]{1,0:T(4,128)S(1)} fusion(bf16[4,32,128]{2,1,0:T(8,128)(2,1)} %param.9), kind=kLoop, calls=%fused_computation.21 | loop fusion | flops 32640 | bytes 33280 | tf_op jit(solution)/shard_map/reduce_sum | solution.py:10
  1.7 0.2 fusion.18
  1.9 0.1 fusion.21
  2.0 0.2 convolution_bitcast_fusion.1
  2.3 15.9 %all_gather.9 = bf16[64,32,32]{0,2,1:T(8,128)(2,1)S(1)} all-gather(bf16[64,4,32]{0,2,1:T(8,128)(2,1)S(1)} %get-tuple-element.11), channel_id=1, replica_groups=mesh['crops'=2,'rows'=4,'chan'=2,'sub'=2] {'rows','sub'}, dimensions={1}, use_global_device_ids=true | all-gather | bytes 147456 | tf_op jit(solution)/shard_map/all_gather | solution.py:66
  18.2 0.8 %copy.58 = bf16[64,32,32]{2,1,0:T(8,128)(2,1)S(1)} copy(bf16[64,32,32]{0,2,1:T(8,128)(2,1)S(1)} %all_gather.9) | data formatting | bytes 262144 | tf_op jit(solution)/shard_map/all_gather | solution.py:66
  19.0 0.1 copy.57
  19.1 0.4 convolution_convert_fusion.1
  19.5 0.1 copy.59
  19.6 0.7 reshape.162
  20.3 3.2 %all-to-all-start = ((bf16[2,2,2048]{2,1,0:T(2,128)(2,1)}), bf16[2,2,2048]{2,1,0:T(2,128)(2,1)S(1)}, u32[]{:S(2)}, u32[]{:S(2)}) async-start(bf16[2,2,2048]{2,1,0:T(2,128)(2,1)} %reshape.162), calls=%async_computation | async-start | bytes 32768 | tf_op jit(solution)/shard_map/all_to_all | solution.py:42
  23.6 0.1 fusion.7
  23.8 0.5 copy-done.5
  24.5 2.9 %all-to-all-done = bf16[2,2,2048]{2,1,0:T(2,128)(2,1)S(1)} async-done(((bf16[2,2,2048]{2,1,0:T(2,128)(2,1)}), bf16[2,2,2048]{2,1,0:T(2,128)(2,1)S(1)}, u32[]{:S(2)}, u32[]{:S(2)}) %all-to-all-start) | async-done | bytes 16416 | tf_op jit(solution)/shard_map/all_to_all | solution.py:42
  27.4 0.1 reshape.163
  27.5 0.1 fusion.60
  27.6 0.2 fusion.63
  27.8 0.1 fusion.66
  28.0 0.1 convert_element_type.92
  28.1 0.7 copy-done.2
  28.8 0.1 fusion.8
  28.9 4.4 %all_gather.10 = bf16[4,32,128]{2,1,0:T(8,128)(2,1)S(1)} all-gather(bf16[4,16,128]{2,1,0:T(8,128)(2,1)S(1)} %fusion.8), channel_id=1, replica_groups=mesh['crops'=2,'rows'=4,'chan'=2,'sub'=2] {'chan'}, dimensions={1}, use_global_device_ids=true | all-gather | bytes 49152 | tf_op jit(solution)/shard_map/all_gather | solution.py:71
  33.4 0.2 fusion.14
  33.6 0.1 fusion.17
  33.7 0.2 convolution_bitcast_fusion
  34.0 0.7 reshape.166
  34.7 4.7 %all-to-all-start.2 = ((bf16[8,2,512]{2,1,0:T(2,128)(2,1)}), bf16[8,2,512]{2,1,0:T(2,128)(2,1)S(1)}, u32[]{:S(2)}, u32[]{:S(2)}) async-start(bf16[8,2,512]{2,1,0:T(2,128)(2,1)} %reshape.166), calls=%async_computation.2 | async-start | bytes 32768 | tf_op jit(solution)/shard_map/all_to_all | solution.py:75
  39.6 0.7 reshape.164
  40.3 4.8 %all-to-all-done.2 = bf16[8,2,512]{2,1,0:T(2,128)(2,1)S(1)} async-done(((bf16[8,2,512]{2,1,0:T(2,128)(2,1)}), bf16[8,2,512]{2,1,0:T(2,128)(2,1)S(1)}, u32[]{:S(2)}, u32[]{:S(2)}) %all-to-all-start.2) | async-done | bytes 16416 | tf_op jit(solution)/shard_map/all_to_all | solution.py:75
  45.1 3.3 %all-to-all-start.1 = ((bf16[8,2,512]{2,1,0:T(2,128)(2,1)}), bf16[8,2,512]{2,1,0:T(2,128)(2,1)S(1)}, u32[]{:S(2)}, u32[]{:S(2)}) async-start(bf16[8,2,512]{2,1,0:T(2,128)(2,1)} %reshape.164), calls=%async_computation.1 | async-start | bytes 32768 | tf_op jit(solution)/shard_map/all_to_all | solution.py:74
  48.4 0.1 reshape.167
  48.5 14.7 %all_gather.11 = bf16[64,32,32]{0,1,2:T(8,128)(2,1)S(1)} all-gather(bf16[64,32,4]{0,1,2:T(8,128)(2,1)S(1)} %bitcast.191), channel_id=1, replica_groups=mesh['crops'=2,'rows'=4,'chan'=2,'sub'=2] {'rows','sub'}, dimensions={2}, use_global_device_ids=true | all-gather | bytes 147456 | tf_op jit(solution)/shard_map/all_gather | solution.py:80
  63.2 0.8 %copy.68 = bf16[64,32,32]{1,2,0:T(8,128)(2,1)S(1)} copy(bf16[64,32,32]{0,1,2:T(8,128)(2,1)S(1)} %all_gather.11) | data formatting | bytes 262144 | tf_op jit(solution)/shard_map/all_gather | solution.py:80
  64.0 0.1 reshape.165
  64.1 0.1 copy.67
  64.2 0.4 convolution_convert_fusion
  64.6 0.1 copy.69
  64.7 0.7 reshape.168
  65.4 3.2 %all-to-all-start.3 = ((bf16[2,2,2048]{2,1,0:T(2,128)(2,1)}), bf16[2,2,2048]{2,1,0:T(2,128)(2,1)S(1)}, u32[]{:S(2)}, u32[]{:S(2)}) async-start(bf16[2,2,2048]{2,1,0:T(2,128)(2,1)} %reshape.168), calls=%async_computation.3 | async-start | bytes 32768 | tf_op jit(solution)/shard_map/all_to_all | solution.py:42
  68.7 0.1 fusion.3
  68.8 3.7 %all-to-all-done.3 = bf16[2,2,2048]{2,1,0:T(2,128)(2,1)S(1)} async-done(((bf16[2,2,2048]{2,1,0:T(2,128)(2,1)}), bf16[2,2,2048]{2,1,0:T(2,128)(2,1)S(1)}, u32[]{:S(2)}, u32[]{:S(2)}) %all-to-all-start.3) | async-done | bytes 16416 | tf_op jit(solution)/shard_map/all_to_all | solution.py:42
  72.5 0.1 reshape.169
  72.6 0.1 fusion.52
  72.7 0.2 fusion.55
  72.9 0.1 fusion.58
  73.1 0.1 convert_element_type.104
  73.1 0.7 %fusion.9 = bf16[4,16,128]{2,1,0:T(8,128)(2,1)} fusion(f32[4,16,128]{2,1,0:T(8,128)S(1)} %fusion.3, bf16[128,4,16]{0,2,1:T(8,128)(2,1)S(1)} %convert_element_type.104, bf16[2,128,128]{2,1,0:T(8,128)(2,1)S(1)} %copy-done.2, bf16[4,16,128]{2,1,0:T(8,128)(2,1)S(1)} %fusion.8), kind=kOutput, calls=%fused_computation.17 | convolution fusion | flops 2129920 | bytes 114688 | tf_op jit(solution)/shard_map/hij,hc->ijc/dot_general | solution.py:48
  (44 shorter events, 1.0 us)
Async XLA Ops:
  0.0 0.7 copy-start.8
  0.0 1.9 %copy-start.3 = (f32[2,128]{1,0:T(2,128)S(1)}, f32[2,128]{1,0:T(2,128)}, u32[]{:S(2)}) copy-start(f32[2,128]{1,0:T(2,128)} %param.12) | copy-start | bytes 3076
  0.0 1.9 %copy-start.4 = (f32[2,128]{1,0:T(2,128)S(1)}, f32[2,128]{1,0:T(2,128)}, u32[]{:S(2)}) copy-start(f32[2,128]{1,0:T(2,128)} %param.11) | copy-start | bytes 3076
  0.0 1.7 %copy-start = (bf16[4,32,128]{2,1,0:T(8,128)(2,1)S(1)}, bf16[4,32,128]{2,1,0:T(8,128)(2,1)}, u32[]{:S(2)}) copy-start(bf16[4,32,128]{2,1,0:T(8,128)(2,1)} %param.9) | copy-start | bytes 98308
  0.0 2.0 %copy-start.1 = (bf16[2,4,128,64]{2,3,1,0:T(8,128)(2,1)S(1)}, bf16[2,4,128,64]{2,3,1,0:T(8,128)(2,1)}, u32[]{:S(2)}) copy-start(bf16[2,4,128,64]{2,3,1,0:T(8,128)(2,1)} %param.13) | copy-start | bytes 393220
  19.6 4.0 %copy-start.7 = (bf16[2,128,128]{2,1,0:T(8,128)(2,1)S(1)}, bf16[2,128,128]{2,1,0:T(8,128)(2,1)}, u32[]{:S(2)}) copy-start(bf16[2,128,128]{2,1,0:T(8,128)(2,1)} %param.14) | copy-start | bytes 196612
  20.3 7.1 %all-to-all-start = ((bf16[2,2,2048]{2,1,0:T(2,128)(2,1)}), bf16[2,2,2048]{2,1,0:T(2,128)(2,1)S(1)}, u32[]{:S(2)}, u32[]{:S(2)}) async-start(bf16[2,2,2048]{2,1,0:T(2,128)(2,1)} %reshape.162), calls=%async_computation | async-start | bytes 32768 | tf_op jit(solution)/shard_map/all_to_all | solution.py:42
  23.6 0.7 copy-start.5
  23.6 0.7 copy-start.6
  27.9 0.8 %copy-start.2 = (bf16[2,128,128]{2,1,0:T(8,128)(2,1)S(1)}, bf16[2,128,128]{2,1,0:T(8,128)(2,1)}, u32[]{:S(2)}) copy-start(bf16[2,128,128]{2,1,0:T(8,128)(2,1)} %param.17) | copy-start | bytes 196612
  34.7 10.3 %all-to-all-start.2 = ((bf16[8,2,512]{2,1,0:T(2,128)(2,1)}), bf16[8,2,512]{2,1,0:T(2,128)(2,1)S(1)}, u32[]{:S(2)}, u32[]{:S(2)}) async-start(bf16[8,2,512]{2,1,0:T(2,128)(2,1)} %reshape.166), calls=%async_computation.2 | async-start | bytes 32768 | tf_op jit(solution)/shard_map/all_to_all | solution.py:75
  45.1 18.9 %all-to-all-start.1 = ((bf16[8,2,512]{2,1,0:T(2,128)(2,1)}), bf16[8,2,512]{2,1,0:T(2,128)(2,1)S(1)}, u32[]{:S(2)}, u32[]{:S(2)}) async-start(bf16[8,2,512]{2,1,0:T(2,128)(2,1)} %reshape.164), calls=%async_computation.1 | async-start | bytes 32768 | tf_op jit(solution)/shard_map/all_to_all | solution.py:74
  65.4 7.1 %all-to-all-start.3 = ((bf16[2,2,2048]{2,1,0:T(2,128)(2,1)}), bf16[2,2,2048]{2,1,0:T(2,128)(2,1)S(1)}, u32[]{:S(2)}, u32[]{:S(2)}) async-start(bf16[2,2,2048]{2,1,0:T(2,128)(2,1)} %reshape.168), calls=%async_computation.3 | async-start | bytes 32768 | tf_op jit(solution)/shard_map/all_to_all | solution.py:42
where the time goes:
time: 74.4 us; the launch traced here: 73.9 us
  blocking collectives  35 us (47%)
  starting transfers between devices  14.5 us (19%)
  waiting for transfers between devices  11.4 us (15%)
  local copies, waits for them, and re-layouts  7.84 us (11%)
  other arithmetic  2.48 us (3%)
  matrix products  2.32 us (3%)
    all_gather x1, blocking collectives, shards(): lax.all_gather(right_edges, ('rows', 'sub'), axis=1, tiled=True)  15.9 us
    all_gather x1, blocking collectives, shards(): lax.all_gather(right_cols, ('rows', 'sub'), axis=2, tiled=True)  14.7 us
    all_to_all x2, waiting for transfers between devices, finish(): lax.all_to_all(triangle, 'chan', split_axis=2, concat_axis=0, tiled=True)  6.63 us
    all_to_all x2, starting transfers between devices, finish(): lax.all_to_all(triangle, 'chan', split_axis=2, concat_axis=0, tiled=True)  6.47 us
    unnamed x26, local copies, waits for them, and re-layouts  5.09 us
    all_to_all x1, waiting for transfers between devices, shards(): lax.all_to_all(right_edges, ('rows', 'sub'), split_axis=2, concat_axis=1,...  4.77 us
    all_to_all x1, starting transfers between devices, shards(): lax.all_to_all(right_edges, ('rows', 'sub'), split_axis=2, concat_axis=1,...  4.68 us
    all_gather x1, blocking collectives, shards(): full_rows = lax.all_gather(layer_one, 'chan', axis=1, tiled=True)  4.4 us
  transfers between devices with their start and end apart: 4, of which 3 were waited for; matrix products, arithmetic and copies ran while one was open for 3% of the time, Pallas kernels for 0%

commit v1 on v0

--- a/solution.py
+++ b/solution.py
@@ -4,6 +4,30 @@
 from jax.sharding import PartitionSpec as P
 
 epsilon = 1e-05
+
+
+def on_each_block(array, axis, dim, work, out_dim):
+    size, position, extent = (lax.axis_size(axis), lax.axis_index(axis), array.shape[dim])
+    right = [(i, (i + 1) % size) for i in range(size)]
+    backward = [(b, a) for a, b in right]
+    lower, upper = (lax.ppermute(array, axis, right), lax.ppermute(array, axis, backward))
+    made = work(array, position * extent)
+    length = made.shape[out_dim]
+    out = jnp.zeros((*made.shape[:out_dim], size * length, *made.shape[out_dim + 1 :]), made.dtype)
+
+    def put(out, made, owner):
+        return lax.dynamic_update_slice_in_dim(out, made, owner * length, axis=out_dim)
+
+    out = put(out, made, position)
+    for lap in range(1, size // 2 + 1):
+        below, above = ((position - lap) % size, (position + lap) % size)
+        carried = (lower, upper)
+        if lap < size // 2:
+            lower, upper = (lax.ppermute(lower, axis, right), lax.ppermute(upper, axis, backward))
+        out = put(out, work(carried[0], below * extent), below)
+        if 2 * lap < size:
+            out = put(out, work(carried[1], above * extent), above)
+    return out
 
 
 def normalize(values, reduce_axis):
@@ -74,11 +98,14 @@
         lax.all_to_all(left_edges, ("rows", "sub"), split_axis=2, concat_axis=1, tiled=True),
         lax.all_to_all(right_edges, ("rows", "sub"), split_axis=2, concat_axis=1, tiled=True),
     )
-    triangle = jnp.einsum(
-        "hki,hkj->hij",
-        left_cols,
-        lax.all_gather(right_cols, ("rows", "sub"), axis=2, tiled=True),
-        preferred_element_type=jnp.float32,
+    triangle = on_each_block(
+        right_cols,
+        ("rows", "sub"),
+        2,
+        lambda shard, at: jnp.einsum(
+            "hki,hkj->hij", left_cols, shard, preferred_element_type=jnp.float32
+        ),
+        2,
     )
     return finish(triangle.astype(jnp.bfloat16), normed, layer_one, 1)
 

time: 74.4 us -> 86.4 us (1.16)
  waiting for transfers between devices: 11.4 us -> 28.7 us
  blocking collectives: 35 us -> 20.3 us
  starting transfers between devices: 14.5 us -> 22.1 us
  matrix products: 2.32 us -> 3.6 us
    ppermute x0 -> x7, waiting for transfers between devices: none -> 15.6 us  [the longest x3 11.9 us: on_each_block(): lax.ppermute(lower, axis, right)]
    all_gather x1 -> x0, blocking collectives: 14.7 us -> none  [shards(): lax.all_gather(right_cols, ('rows', 'sub'), axis=2, tiled=True)]
    ppermute x0 -> x7, starting transfers between devices: none -> 7.57 us  [the longest x2 3.66 us: on_each_block(): lax.ppermute(upper, axis, backward)]
    all_to_all x1, waiting for transfers between devices: 0.01 us -> 1.56 us  [shards(): lax.all_to_all(left_edges, ('rows', 'sub'), split_axis=2, concat_axis=1,...]
    dot_general x1 -> x8, matrix products: 0.37 us -> 1.65 us  [shards(): jnp.einsum('hki,hkj->hij', left_cols, shard, preferred_element_type=jnp.f...]
    dot_general x0 -> x8, local copies, waits for them, and re-layouts: none -> 0.96 us  [shards(): jnp.einsum('hki,hkj->hij', left_cols, shard, preferred_element_type=jnp.f...]
  transfers between devices with their start and end apart: 4 -> 11, of which waited for: 3 -> 9; matrix products, arithmetic and copies ran while one was open for 3% -> 4% of each run, Pallas kernels for 0% -> 0%
where the time goes in v1:
time: 86.4 us; the launch traced here: 85.8 us
  waiting for transfers between devices  28.7 us (33%)
  starting transfers between devices  22.1 us (26%)
  blocking collectives  20.3 us (23%)
  local copies, waits for them, and re-layouts  8.16 us (9%)
  matrix products  3.6 us (4%)
  other arithmetic  2.48 us (3%)
    all_gather x1, blocking collectives, shards(): lax.all_gather(right_edges, ('rows', 'sub'), axis=1, tiled=True)  15.9 us
    ppermute x3, waiting for transfers between devices, on_each_block(): lax.ppermute(lower, axis, right)  11.9 us
    all_to_all x2, waiting for transfers between devices, finish(): lax.all_to_all(triangle, 'chan', split_axis=2, concat_axis=0, tiled=True)  6.63 us
    all_to_all x2, starting transfers between devices, finish(): lax.all_to_all(triangle, 'chan', split_axis=2, concat_axis=0, tiled=True)  6.47 us
    unnamed x26, local copies, waits for them, and re-layouts  5.09 us
    all_to_all x1, waiting for transfers between devices, shards(): lax.all_to_all(right_edges, ('rows', 'sub'), split_axis=2, concat_axis=1,...  4.93 us
    all_to_all x1, starting transfers between devices, shards(): lax.all_to_all(right_edges, ('rows', 'sub'), split_axis=2, concat_axis=1,...  4.68 us
    all_gather x1, blocking collectives, shards(): full_rows = lax.all_gather(layer_one, 'chan', axis=1, tiled=True)  4.4 us
  transfers between devices with their start and end apart: 11, of which 9 were waited for; matrix products, arithmetic and copies ran while one was open for 4% of the time, Pallas kernels for 0%

profile of v1, /device:TPU:0, one launch (start us, length us, event | category | flops | bytes accessed | tf_op | source)
XLA Modules:
  0.0 85.8 jit_solution(1064110318421829122)
XLA Ops:
  0.0 0.6 copy-done.8
  0.8 0.8 convert_reduce_fusion.1
  1.7 0.2 fusion.18
  2.0 0.2 convolution_bitcast_fusion.1
  2.3 15.9 %all_gather.6 = bf16[64,32,32]{0,2,1:T(8,128)(2,1)S(1)} all-gather(bf16[64,4,32]{0,2,1:T(8,128)(2,1)S(1)} %get-tuple-element.11), channel_id=1, replica_groups=mesh['crops'=2,'rows'=4,'chan'=2,'sub'=2] {'rows','sub'}, dimensions={1}, use_global_device_ids=true | all-gather | bytes 147456 | tf_op jit(solution)/shard_map/all_gather | solution.py:90
  18.2 0.8 copy.87
  19.1 0.4 convolution_convert_fusion
  19.6 0.7 reshape.162
  20.3 3.2 %all-to-all-start = ((bf16[2,2,2048]{2,1,0:T(2,128)(2,1)}), bf16[2,2,2048]{2,1,0:T(2,128)(2,1)S(1)}, u32[]{:S(2)}, u32[]{:S(2)}) async-start(bf16[2,2,2048]{2,1,0:T(2,128)(2,1)} %reshape.162), calls=%async_computation | async-start | bytes 32768 | tf_op jit(solution)/shard_map/all_to_all | solution.py:66
  23.6 0.1 fusion.7
  23.8 0.5 copy-done.5
  24.5 2.9 %all-to-all-done = bf16[2,2,2048]{2,1,0:T(2,128)(2,1)S(1)} async-done(((bf16[2,2,2048]{2,1,0:T(2,128)(2,1)}), bf16[2,2,2048]{2,1,0:T(2,128)(2,1)S(1)}, u32[]{:S(2)}, u32[]{:S(2)}) %all-to-all-start) | async-done | bytes 16416 | tf_op jit(solution)/shard_map/all_to_all | solution.py:66
  27.6 0.2 fusion.63
  28.1 0.7 copy-done.2
  28.8 0.1 fusion.8
  28.9 4.4 %all_gather.7 = bf16[4,32,128]{2,1,0:T(8,128)(2,1)S(1)} all-gather(bf16[4,16,128]{2,1,0:T(8,128)(2,1)S(1)} %fusion.8), channel_id=1, replica_groups=mesh['crops'=2,'rows'=4,'chan'=2,'sub'=2] {'chan'}, dimensions={1}, use_global_device_ids=true | all-gather | bytes 49152 | tf_op jit(solution)/shard_map/all_gather | solution.py:95
  33.4 0.2 fusion.14
  33.7 0.2 convolution_bitcast_fusion
  34.0 0.7 reshape.166
  34.7 4.7 %all-to-all-start.2 = ((bf16[8,2,512]{2,1,0:T(2,128)(2,1)}), bf16[8,2,512]{2,1,0:T(2,128)(2,1)S(1)}, u32[]{:S(2)}, u32[]{:S(2)}) async-start(bf16[8,2,512]{2,1,0:T(2,128)(2,1)} %reshape.166), calls=%async_computation.2 | async-start | bytes 32768 | tf_op jit(solution)/shard_map/all_to_all | solution.py:99
  39.4 0.7 reshape.164
  40.1 4.9 %all-to-all-done.2 = bf16[8,2,512]{2,1,0:T(2,128)(2,1)S(1)} async-done(((bf16[8,2,512]{2,1,0:T(2,128)(2,1)}), bf16[8,2,512]{2,1,0:T(2,128)(2,1)S(1)}, u32[]{:S(2)}, u32[]{:S(2)}) %all-to-all-start.2) | async-done | bytes 16416 | tf_op jit(solution)/shard_map/all_to_all | solution.py:99
  45.1 3.3 %all-to-all-start.1 = ((bf16[8,2,512]{2,1,0:T(2,128)(2,1)}), bf16[8,2,512]{2,1,0:T(2,128)(2,1)S(1)}, u32[]{:S(2)}, u32[]{:S(2)}) async-start(bf16[8,2,512]{2,1,0:T(2,128)(2,1)} %reshape.164), calls=%async_computation.1 | async-start | bytes 32768 | tf_op jit(solution)/shard_map/all_to_all | solution.py:98
  48.9 0.3 collective-permute-start
  49.3 3.3 %collective-permute-start.1 = (bf16[64,32,4]{1,2,0:T(4,128)(2,1)S(1)}, bf16[64,32,4]{1,2,0:T(4,128)(2,1)S(1)}, u32[]{:S(2)}, u32[]{:S(2)}) collective-permute-start(bf16[64,32,4]{1,2,0:T(4,128)(2,1)S(1)} %copy.97), channel_id=1, source_target_pairs={{1,0},{4,1},{5,4},{8,5},{9,8},{12,9},{13,12},{0,13},{3,2},{6,3},{7... | collective-permute-start | bytes 49160 | tf_op jit(solution)/shard_map/ppermute | solution.py:13
  52.5 1.6 %all-to-all-done.1 = bf16[8,2,512]{2,1,0:T(2,128)(2,1)S(1)} async-done(((bf16[8,2,512]{2,1,0:T(2,128)(2,1)}), bf16[8,2,512]{2,1,0:T(2,128)(2,1)S(1)}, u32[]{:S(2)}, u32[]{:S(2)}) %all-to-all-start.1) | async-done | bytes 16416 | tf_op jit(solution)/shard_map/all_to_all | solution.py:98
  54.3 0.2 fusion.84
  54.7 0.2 fusion.86
  55.0 0.2 fusion.85
  55.4 3.4 %collective-permute-start.3 = (bf16[64,32,4]{1,2,0:T(4,128)(2,1)S(1)}, bf16[64,32,4]{1,2,0:T(4,128)(2,1)S(1)}, u32[]{:S(2)}, u32[]{:S(2)}) collective-permute-start(bf16[64,32,4]{1,2,0:T(4,128)(2,1)S(1)} %collective-permute-done.1), channel_id=1, source_target_pairs={{1,0},{4,1},{5,4},{8,5},{9,8},{12,9},{13,12},{0,13},{3,2},{6,3},{7... | collective-permute-start | bytes 49160 | tf_op jit(solution)/shard_map/ppermute | solution.py:26
  58.7 1.9 %collective-permute-done.3 = bf16[64,32,4]{1,2,0:T(4,128)(2,1)S(1)} collective-permute-done((bf16[64,32,4]{1,2,0:T(4,128)(2,1)S(1)}, bf16[64,32,4]{1,2,0:T(4,128)(2,1)S(1)}, u32[]{:S(2)}, u32[]{:S(2)}) %collective-permute-start.3) | collective-permute-done | bytes 16416 | tf_op jit(solution)/shard_map/ppermute | solution.py:26
  60.6 0.2 fusion.88
  61.0 3.3 %collective-permute-done.2 = bf16[64,32,4]{1,2,0:T(4,128)(2,1)S(1)} collective-permute-done((bf16[64,32,4]{1,2,0:T(4,128)(2,1)S(1)}, bf16[64,32,4]{1,2,0:T(4,128)(2,1)S(1)}, u32[]{:S(2)}, u32[]{:S(2)}) %collective-permute-start.2) | collective-permute-done | bytes 16416 | tf_op jit(solution)/shard_map/ppermute | solution.py:26
  64.3 0.2 fusion.87
  64.6 0.3 collective-permute-start.5
  65.0 0.3 collective-permute-start.4
  65.2 1.8 %collective-permute-done.5 = bf16[64,32,4]{1,2,0:T(4,128)(2,1)S(1)} collective-permute-done((bf16[64,32,4]{1,2,0:T(4,128)(2,1)S(1)}, bf16[64,32,4]{1,2,0:T(4,128)(2,1)S(1)}, u32[]{:S(2)}, u32[]{:S(2)}) %collective-permute-start.5) | collective-permute-done | bytes 16416 | tf_op jit(solution)/shard_map/ppermute | solution.py:26
  67.0 0.2 fusion.90
  67.3 3.1 %collective-permute-done.4 = bf16[64,32,4]{1,2,0:T(4,128)(2,1)S(1)} collective-permute-done((bf16[64,32,4]{1,2,0:T(4,128)(2,1)S(1)}, bf16[64,32,4]{1,2,0:T(4,128)(2,1)S(1)}, u32[]{:S(2)}, u32[]{:S(2)}) %collective-permute-start.4) | collective-permute-done | bytes 16416 | tf_op jit(solution)/shard_map/ppermute | solution.py:26
  70.5 0.2 fusion.89
  70.9 5.5 %collective-permute-done.6 = bf16[64,32,4]{1,2,0:T(4,128)(2,1)S(1)} collective-permute-done((bf16[64,32,4]{1,2,0:T(4,128)(2,1)S(1)}, bf16[64,32,4]{1,2,0:T(4,128)(2,1)S(1)}, u32[]{:S(2)}, u32[]{:S(2)}) %collective-permute-start.6) | collective-permute-done | bytes 16416 | tf_op jit(solution)/shard_map/ppermute | solution.py:26
  76.3 0.2 fusion.91
  76.7 0.7 reshape.168
  77.4 3.2 %all-to-all-start.3 = ((bf16[2,2,2048]{2,1,0:T(2,128)(2,1)}), bf16[2,2,2048]{2,1,0:T(2,128)(2,1)S(1)}, u32[]{:S(2)}, u32[]{:S(2)}) async-start(bf16[2,2,2048]{2,1,0:T(2,128)(2,1)} %reshape.168), calls=%async_computation.3 | async-start | bytes 32768 | tf_op jit(solution)/shard_map/all_to_all | solution.py:66
  80.6 0.1 fusion.3
  80.8 3.7 %all-to-all-done.3 = bf16[2,2,2048]{2,1,0:T(2,128)(2,1)S(1)} async-done(((bf16[2,2,2048]{2,1,0:T(2,128)(2,1)}), bf16[2,2,2048]{2,1,0:T(2,128)(2,1)S(1)}, u32[]{:S(2)}, u32[]{:S(2)}) %all-to-all-start.3) | async-done | bytes 16416 | tf_op jit(solution)/shard_map/all_to_all | solution.py:66
  84.7 0.2 fusion.55
  85.1 0.7 fusion.9
  (80 shorter events, 3.8 us)
Async XLA Ops:
  0.0 0.7 copy-start.8
  0.0 1.9 %copy-start.3 = (f32[2,128]{1,0:T(2,128)S(1)}, f32[2,128]{1,0:T(2,128)}, u32[]{:S(2)}) copy-start(f32[2,128]{1,0:T(2,128)} %param.12) | copy-start | bytes 3076
  0.0 1.9 %copy-start.4 = (f32[2,128]{1,0:T(2,128)S(1)}, f32[2,128]{1,0:T(2,128)}, u32[]{:S(2)}) copy-start(f32[2,128]{1,0:T(2,128)} %param.11) | copy-start | bytes 3076
  0.0 1.7 %copy-start = (bf16[4,32,128]{2,1,0:T(8,128)(2,1)S(1)}, bf16[4,32,128]{2,1,0:T(8,128)(2,1)}, u32[]{:S(2)}) copy-start(bf16[4,32,128]{2,1,0:T(8,128)(2,1)} %param.9) | copy-start | bytes 98308
  0.0 2.0 %copy-start.1 = (bf16[2,4,128,64]{2,3,1,0:T(8,128)(2,1)S(1)}, bf16[2,4,128,64]{2,3,1,0:T(8,128)(2,1)}, u32[]{:S(2)}) copy-start(bf16[2,4,128,64]{2,3,1,0:T(8,128)(2,1)} %param.13) | copy-start | bytes 393220
  19.6 4.0 %copy-start.7 = (bf16[2,128,128]{2,1,0:T(8,128)(2,1)S(1)}, bf16[2,128,128]{2,1,0:T(8,128)(2,1)}, u32[]{:S(2)}) copy-start(bf16[2,128,128]{2,1,0:T(8,128)(2,1)} %param.14) | copy-start | bytes 196612
  20.3 7.1 %all-to-all-start = ((bf16[2,2,2048]{2,1,0:T(2,128)(2,1)}), bf16[2,2,2048]{2,1,0:T(2,128)(2,1)S(1)}, u32[]{:S(2)}, u32[]{:S(2)}) async-start(bf16[2,2,2048]{2,1,0:T(2,128)(2,1)} %reshape.162), calls=%async_computation | async-start | bytes 32768 | tf_op jit(solution)/shard_map/all_to_all | solution.py:66
  23.6 0.7 copy-start.5
  23.6 0.7 copy-start.6
  27.9 0.8 copy-start.2
  34.7 10.3 %all-to-all-start.2 = ((bf16[8,2,512]{2,1,0:T(2,128)(2,1)}), bf16[8,2,512]{2,1,0:T(2,128)(2,1)S(1)}, u32[]{:S(2)}, u32[]{:S(2)}) async-start(bf16[8,2,512]{2,1,0:T(2,128)(2,1)} %reshape.166), calls=%async_computation.2 | async-start | bytes 32768 | tf_op jit(solution)/shard_map/all_to_all | solution.py:99
  45.1 9.0 %all-to-all-start.1 = ((bf16[8,2,512]{2,1,0:T(2,128)(2,1)}), bf16[8,2,512]{2,1,0:T(2,128)(2,1)S(1)}, u32[]{:S(2)}, u32[]{:S(2)}) async-start(bf16[8,2,512]{2,1,0:T(2,128)(2,1)} %reshape.164), calls=%async_computation.1 | async-start | bytes 32768 | tf_op jit(solution)/shard_map/all_to_all | solution.py:98
  48.9 6.1 %collective-permute-start = (bf16[64,32,4]{1,2,0:T(4,128)(2,1)S(1)}, bf16[64,32,4]{1,2,0:T(4,128)(2,1)S(1)}, u32[]{:S(2)}, u32[]{:S(2)}) collective-permute-start(bf16[64,32,4]{1,2,0:T(4,128)(2,1)S(1)} %copy.97), channel_id=1, source_target_pairs={{0,1},{1,4},{4,5},{5,8},{8,9},{9,12},{12,13},{13,0},{2,3},{3,6},{6... | collective-permute-start | bytes 49160 | tf_op jit(solution)/shard_map/ppermute | solution.py:13
  49.3 5.4 %collective-permute-start.1 = (bf16[64,32,4]{1,2,0:T(4,128)(2,1)S(1)}, bf16[64,32,4]{1,2,0:T(4,128)(2,1)S(1)}, u32[]{:S(2)}, u32[]{:S(2)}) collective-permute-start(bf16[64,32,4]{1,2,0:T(4,128)(2,1)S(1)} %copy.97), channel_id=1, source_target_pairs={{1,0},{4,1},{5,4},{8,5},{9,8},{12,9},{13,12},{0,13},{3,2},{6,3},{7... | collective-permute-start | bytes 49160 | tf_op jit(solution)/shard_map/ppermute | solution.py:13
  55.4 5.3 %collective-permute-start.3 = (bf16[64,32,4]{1,2,0:T(4,128)(2,1)S(1)}, bf16[64,32,4]{1,2,0:T(4,128)(2,1)S(1)}, u32[]{:S(2)}, u32[]{:S(2)}) collective-permute-start(bf16[64,32,4]{1,2,0:T(4,128)(2,1)S(1)} %collective-permute-done.1), channel_id=1, source_target_pairs={{1,0},{4,1},{5,4},{8,5},{9,8},{12,9},{13,12},{0,13},{3,2},{6,3},{7... | collective-permute-start | bytes 49160 | tf_op jit(solution)/shard_map/ppermute | solution.py:26
  58.7 5.6 %collective-permute-start.2 = (bf16[64,32,4]{1,2,0:T(4,128)(2,1)S(1)}, bf16[64,32,4]{1,2,0:T(4,128)(2,1)S(1)}, u32[]{:S(2)}, u32[]{:S(2)}) collective-permute-start(bf16[64,32,4]{1,2,0:T(4,128)(2,1)S(1)} %collective-permute-done), channel_id=1, source_target_pairs={{0,1},{1,4},{4,5},{5,8},{8,9},{9,12},{12,13},{13,0},{2,3},{3,6},{6... | collective-permute-start | bytes 49160 | tf_op jit(solution)/shard_map/ppermute | solution.py:26
  64.6 2.4 %collective-permute-start.5 = (bf16[64,32,4]{1,2,0:T(4,128)(2,1)S(1)}, bf16[64,32,4]{1,2,0:T(4,128)(2,1)S(1)}, u32[]{:S(2)}, u32[]{:S(2)}) collective-permute-start(bf16[64,32,4]{1,2,0:T(4,128)(2,1)S(1)} %collective-permute-done.3), channel_id=1, source_target_pairs={{1,0},{4,1},{5,4},{8,5},{9,8},{12,9},{13,12},{0,13},{3,2},{6,3},{7... | collective-permute-start | bytes 49160 | tf_op jit(solution)/shard_map/ppermute | solution.py:26
  65.0 5.5 %collective-permute-start.4 = (bf16[64,32,4]{1,2,0:T(4,128)(2,1)S(1)}, bf16[64,32,4]{1,2,0:T(4,128)(2,1)S(1)}, u32[]{:S(2)}, u32[]{:S(2)}) collective-permute-start(bf16[64,32,4]{1,2,0:T(4,128)(2,1)S(1)} %collective-permute-done.2), channel_id=1, source_target_pairs={{0,1},{1,4},{4,5},{5,8},{8,9},{9,12},{12,13},{13,0},{2,3},{3,6},{6... | collective-permute-start | bytes 49160 | tf_op jit(solution)/shard_map/ppermute | solution.py:26
  70.8 5.5 %collective-permute-start.6 = (bf16[64,32,4]{1,2,0:T(4,128)(2,1)S(1)}, bf16[64,32,4]{1,2,0:T(4,128)(2,1)S(1)}, u32[]{:S(2)}, u32[]{:S(2)}) collective-permute-start(bf16[64,32,4]{1,2,0:T(4,128)(2,1)S(1)} %collective-permute-done.4), channel_id=1, source_target_pairs={{0,1},{1,4},{4,5},{5,8},{8,9},{9,12},{12,13},{13,0},{2,3},{3,6},{6... | collective-permute-start | bytes 49160 | tf_op jit(solution)/shard_map/ppermute | solution.py:26
  77.4 7.1 %all-to-all-start.3 = ((bf16[2,2,2048]{2,1,0:T(2,128)(2,1)}), bf16[2,2,2048]{2,1,0:T(2,128)(2,1)S(1)}, u32[]{:S(2)}, u32[]{:S(2)}) async-start(bf16[2,2,2048]{2,1,0:T(2,128)(2,1)} %reshape.168), calls=%async_computation.3 | async-start | bytes 32768 | tf_op jit(solution)/shard_map/all_to_all | solution.py:66
